TPU v7x, 512 devices: a whole 4x4x16 slice. The times are simulated.
512 devices in a mesh: vocab: 16 (over z_hi, x, core), seq: 32 (over z_lo, y).
Axes of the slice: x: 4, y: 4, z: 16 (z_hi: 2, z_lo: 8; z = z_hi * 8 + z_lo), core: 2. Of those that a mesh axis runs over, the one named last changes fastest.
Arguments:
- token_ids: int32 [2, 2048], P(None, 'seq'), may hold values from 0 to 131071
- keep_mask: int32 [2, 2048], P(None, 'seq'), may hold values 0 or 1
- target_length: int32 [2], replicated, may hold values from 256 to 2048, as said below
- source_length: int32 [2], replicated, may hold values from 128 to 1024, as said below
- embed_table: bfloat16 [131072, 4096], P('vocab', 'seq'), may hold values from -6 to 6
- self_gain: float32 [4096], replicated, may hold values from 0.1 to 1.9
- query_weight: bfloat16 [4096, 2048], P('seq', 'vocab'), may hold values from -0.03125 to 0.03125
- key_weight: bfloat16 [4096, 2048], P('seq', 'vocab'), may hold values from -6 to 6
- value_weight: bfloat16 [4096, 2048], P('seq', 'vocab'), may hold values from -0.09375 to 0.09375
- self_out_weight: bfloat16 [2048, 4096], P('vocab'), may hold values from -0.5 to 0.5
- cross_gain: float32 [4096], replicated, may hold values from 0.1 to 1.9
- cross_query_weight: bfloat16 [4096, 2048], P('seq', 'vocab'), may hold values from -0.03125 to 0.03125
- cross_keys: bfloat16 [2, 1024, 2048], P(None, 'seq', 'vocab'), may hold values from -24 to 24
- cross_values: bfloat16 [2, 1024, 2048], P(None, 'seq', 'vocab'), may hold values from -6 to 6
- cross_out_weight: bfloat16 [2048, 4096], P('vocab'), may hold values from -0.375 to 0.375
Outputs:
- layer_output: bfloat16 [2, 2048, 4096], P(None, 'seq', 'vocab')
Inputs may be any that keep to these rules, and one draw needn't show every extreme that they name: `target_length`: the pairs' lengths all differ, and one pair has length 2048. `source_length`: the pairs' lengths all differ, and one pair has length 1024.
All inputs are finite; a program needn't handle non-finite values. No bound on the sum of `keep_mask` on one device may be relied on, other than what follows from the above.
Results may differ from a plain program's by a relative error of at most 0.035.
Values may be sent and summed in bfloat16 or wider, within the bound.
A program may use at most 64 MiB of HBM per device.

v0:
```python
import jax
import jax.numpy as jnp
from jax import lax
from jax.sharding import PartitionSpec as P

DH = 64


def rms_scale(values, gain):
    return values * lax.rsqrt(jnp.mean(values * values, axis=-1, keepdims=True) + 1e-06) * gain


def attend(query, keys, values, visible):
    pair_count = query.shape[0]
    query_rows = query.shape[1]
    head_count = query.shape[2] // DH
    q_heads = query.reshape(pair_count, query_rows, head_count, DH)
    k_heads = keys.reshape(pair_count, keys.shape[1], head_count, DH)
    v_heads = values.reshape(pair_count, values.shape[1], head_count, DH)
    scores = jnp.einsum("pqhd,pkhd->phqk", q_heads, k_heads, preferred_element_type=jnp.float32)
    scores = jnp.where(visible[:, None, :, :], scores, -jnp.inf)
    raised = jnp.exp(scores - jnp.max(scores, axis=-1, keepdims=True))
    totals = jnp.sum(raised, axis=-1)
    mixed = jnp.einsum(
        "phqk,pkhd->pqhd", raised.astype(jnp.bfloat16), v_heads, preferred_element_type=jnp.float32
    )
    mixed = mixed / jnp.transpose(totals, (0, 2, 1))[:, :, :, None]
    return mixed.reshape(pair_count, query_rows, head_count * DH).astype(jnp.bfloat16)


def row_fold(source, portion):
    return jnp.dot(source, portion, preferred_element_type=jnp.float32)


def on_device(
    token_ids,
    keep_mask,
    target_length,
    source_length,
    embed_table,
    self_gain,
    query_weight,
    key_weight,
    value_weight,
    self_out_weight,
    cross_gain,
    cross_query_weight,
    cross_keys,
    cross_values,
    cross_out_weight,
):
    seq_count = lax.axis_size("seq")
    seq_index = lax.axis_index("seq")
    vocab_index = lax.axis_index("vocab")
    vocab_count = lax.axis_size("vocab")
    every_id = lax.all_gather(token_ids, "seq", axis=1, tiled=True)
    shard_rows = embed_table.shape[0]
    local_ids = every_id - vocab_index * shard_rows
    inside = (local_ids >= 0) & (local_ids < shard_rows)
    picked = jnp.take(embed_table, jnp.clip(local_ids, 0, shard_rows - 1).reshape(-1), axis=0)
    picked = picked.reshape(every_id.shape[0], every_id.shape[1], embed_table.shape[1])
    partial_rows = jnp.where(inside[:, :, None], picked, jnp.zeros_like(picked))
    arrived = lax.all_to_all(partial_rows, "seq", split_axis=1, concat_axis=2, tiled=True)
    summed = lax.psum(arrived.astype(jnp.float32).astype(jnp.bfloat16), "vocab").astype(jnp.float32)
    embedded_pairs = summed * keep_mask.astype(jnp.float32)[:, :, None]
    pair_count = embedded_pairs.shape[0]
    token_rows = embedded_pairs.shape[1]
    model_cols = embedded_pairs.shape[2]
    flat_rows = pair_count * token_rows
    embedded = embedded_pairs.reshape(flat_rows, model_cols)
    self_normed = rms_scale(embedded, self_gain).astype(jnp.bfloat16)
    queries = row_fold(self_normed, lax.all_gather(query_weight, "seq", axis=0, tiled=True))
    keys = row_fold(self_normed, lax.all_gather(key_weight, "seq", axis=0, tiled=True))
    values = row_fold(self_normed, lax.all_gather(value_weight, "seq", axis=0, tiled=True))
    head_cols = queries.shape[1]
    queries = queries.astype(jnp.bfloat16).reshape(pair_count, token_rows, head_cols)
    keys = keys.astype(jnp.bfloat16).reshape(pair_count, token_rows, head_cols)
    values = values.astype(jnp.bfloat16).reshape(pair_count, token_rows, head_cols)
    keys_every, values_every = (
        lax.all_gather(keys, "seq", axis=1, tiled=True),
        lax.all_gather(values, "seq", axis=1, tiled=True),
    )
    query_pos = seq_index * token_rows + jnp.arange(token_rows, dtype=jnp.int32)
    key_pos = jnp.arange(token_rows * seq_count, dtype=jnp.int32)
    causal = key_pos[None, :] <= query_pos[:, None]
    visible = causal[None, :, :] & (key_pos[None, None, :] < target_length[:, None, None])
    self_context = attend(queries, keys_every, values_every, visible).reshape(flat_rows, head_cols)
    self_terms = jnp.dot(self_context, self_out_weight, preferred_element_type=jnp.float32)
    share_cols = model_cols // vocab_count
    col_start = vocab_index * share_cols
    after_self = embedded + lax.psum(self_terms.astype(jnp.bfloat16), "vocab").astype(jnp.float32)
    cross_normed = rms_scale(after_self, cross_gain).astype(jnp.bfloat16)
    after_share = lax.dynamic_slice_in_dim(after_self, col_start, share_cols, 1)
    cross_queries = row_fold(
        cross_normed, lax.all_gather(cross_query_weight, "seq", axis=0, tiled=True)
    )
    cross_queries = cross_queries.astype(jnp.bfloat16).reshape(pair_count, token_rows, head_cols)
    source_keys, source_values = (
        lax.all_gather(cross_keys, "seq", axis=1, tiled=True),
        lax.all_gather(cross_values, "seq", axis=1, tiled=True),
    )
    source_pos = jnp.arange(source_keys.shape[1], dtype=jnp.int32)
    cross_visible = jnp.broadcast_to(
        source_pos[None, None, :] < source_length[:, None, None],
        (pair_count, token_rows, source_keys.shape[1]),
    )
    cross_context = attend(cross_queries, source_keys, source_values, cross_visible).reshape(
        flat_rows, head_cols
    )
    cross_terms = jnp.dot(cross_context, cross_out_weight, preferred_element_type=jnp.float32)
    cross_share = lax.psum_scatter(
        cross_terms.astype(jnp.bfloat16), "vocab", scatter_dimension=1, tiled=True
    ).astype(jnp.float32)
    return (
        (after_share + cross_share).reshape(pair_count, token_rows, share_cols).astype(jnp.bfloat16)
    )


def solution(mesh):
    return jax.shard_map(
        on_device,
        mesh=mesh,
        in_specs=(
            P(None, "seq"),
            P(None, "seq"),
            P(),
            P(),
            P("vocab", "seq"),
            P(),
            P("seq", "vocab"),
            P("seq", "vocab"),
            P("seq", "vocab"),
            P("vocab", None),
            P(),
            P("seq", "vocab"),
            P(None, "seq", "vocab"),
            P(None, "seq", "vocab"),
            P("vocab", None),
        ),
        out_specs=P(None, "seq", "vocab"),
        check_vma=False,
    )
```

profile of v0, /device:TPU:8, one launch (start us, length us, event | category | flops | bytes accessed | tf_op | source)
XLA Modules:
  0.0 1701.3 jit_solution(9061207319396813482)
XLA Ops:
  7.4 117.5 %all-gather = s32[32,64,2]{1,2,0:T(2,128)S(1)} all-gather(s32[1,64,2]{1,2,0:T(2,128)} %bitcast.79), channel_id=1, replica_groups=mesh['vocab'=16,'seq'=32] {'seq'}, dimensions={0}, use_global_device_ids=true | all-gather | bytes 16896 | tf_op jit(solution)/shard_map/all_gather | solution.py:56
  124.9 0.1 reshape.202
  125.1 0.5 copy.50
  125.5 0.1 reshape.203
  125.6 1.1 copy.49
  126.7 12.1 gather_fusion
  138.9 10.4 broadcast_select_fusion.1
  149.3 48.0 %all_to_all.18 = bf16[2,2048,128]{2,0,1:T(2,128)(2,1)S(1)} all-to-all(bf16[2,2048,128]{2,0,1:T(2,128)(2,1)S(1)} %broadcast_select_fusion.1), channel_id=1, replica_groups=mesh['vocab'=16,'seq'=32] {'seq'}, dimensions={1} | all-to-all | bytes 2097152 | tf_op jit(solution)/shard_map/all_to_all | solution.py:63
  197.3 0.7 copy.52
  198.0 1.3 all_to_all.16
  199.3 0.0 all-gather.14.cloned.1.call-start
  199.3 0.5 all-gather.14.cloned.1.call-update
  199.9 0.0 all-gather.8.cloned.1.call-start
  199.9 0.5 all-gather.8.cloned.1.call-update
  200.5 0.5 all-gather.12.cloned.1.call-update
  201.0 0.0 all-gather.16.cloned.1.call-start
  201.1 254.8 %all-reduce.3.cloned.1.call-done = bf16[2,64,4096]{2,1,0:T(8,128)(2,1)} async-done(((bf16[2,64,4096]{2,1,0:T(8,128)(2,1)}), bf16[2,64,4096]{2,1,0:T(8,128)(2,1)}) %all-reduce.3.cloned.1.call-update) | async-done | bytes 1048592 | tf_op jit(solution)/shard_map/psum | solution.py:64
  455.9 2.9 multiply_reduce_fusion.1
  458.8 0.1 rsqrt.20
  458.8 1.9 fusion.1
  460.8 2.3 convolution_convert_fusion.3
  463.0 0.0 all-gather.10.cloned.1.call-start
  463.1 179.5 %all-gather.8.cloned.1.call-done = bf16[4096,128]{1,0:T(8,128)(2,1)} async-done(((bf16[128,128]{1,0:T(8,128)(2,1)}), bf16[4096,128]{1,0:T(8,128)(2,1)}) %all-gather.8.cloned.1.call-update) | async-done | bytes 1048592 | tf_op jit(solution)/shard_map/all_gather | solution.py:74
  642.6 2.3 convolution_convert_fusion.5
  644.9 0.0 all-reduce.5.cloned.1.call-start
  645.0 0.1 iota_compare_fusion.1
  645.1 0.1 iota_compare_fusion
  645.2 0.2 broadcast_and_fusion
  645.4 219.1 %all-gather.12.cloned.1.call-done = bf16[4096,128]{1,0:T(8,128)(2,1)} async-done(((bf16[128,128]{1,0:T(8,128)(2,1)}), bf16[4096,128]{1,0:T(8,128)(2,1)}) %all-gather.12.cloned.1.call-update) | async-done | bytes 1048592 | tf_op jit(solution)/shard_map/all_gather | solution.py:72
  864.5 1.6 convolution_convert_fusion.4
  866.2 0.1 reshape_reshape.6
  866.3 220.4 %all-gather.16.cloned.1.call-done = bf16[2,2048,128]{2,1,0:T(8,128)(2,1)} async-done(((bf16[2,64,128]{2,1,0:T(8,128)(2,1)}), bf16[2,2048,128]{2,1,0:T(8,128)(2,1)}) %all-gather.16.cloned.1.call-update) | async-done | bytes 1048592 | tf_op jit(solution)/shard_map/all_gather | solution.py:80
  1086.7 1.5 copy.54
  1088.2 0.6 fusion.19
  1088.8 1.3 copy-done.1
  1090.1 0.4 fusion.2
  1090.5 218.4 %all-gather.10.cloned.1.call-done = bf16[2,2048,128]{2,1,0:T(8,128)(2,1)} async-done(((bf16[2,64,128]{2,1,0:T(8,128)(2,1)}), bf16[2,2048,128]{2,1,0:T(8,128)(2,1)}) %all-gather.10.cloned.1.call-update) | async-done | bytes 1048592 | tf_op jit(solution)/shard_map/all_gather | solution.py:81
  1308.9 1.5 copy.53
  1310.4 2.1 fusion.7
  1312.5 0.1 copy.56
  1312.6 0.1 convert_element_type.72
  1312.7 2.6 convolution_convert_fusion.1
  1315.4 0.0 all-gather.18.cloned.1.call-start
  1315.4 0.7 all-gather.18.cloned.1.call-update
  1316.1 0.0 reduce-scatter.2.cloned.1.call-start
  1316.2 116.6 %all_gather.34 = bf16[2,1024,128]{2,1,0:T(8,128)(2,1)S(1)} all-gather(bf16[2,32,128]{2,1,0:T(8,128)(2,1)S(1)} %copy-done.6), channel_id=1, replica_groups=mesh['vocab'=16,'seq'=32] {'seq'}, dimensions={1}, use_global_device_ids=true | all-gather | bytes 540672 | tf_op jit(solution)/shard_map/all_gather | solution.py:99
  1432.8 0.2 copy.57
  1433.0 123.8 %all_gather.35 = bf16[2,1024,128]{2,1,0:T(8,128)(2,1)S(1)} all-gather(bf16[2,32,128]{2,1,0:T(8,128)(2,1)S(1)} %copy-done.7), channel_id=1, replica_groups=mesh['vocab'=16,'seq'=32] {'seq'}, dimensions={1}, use_global_device_ids=true | all-gather | bytes 540672 | tf_op jit(solution)/shard_map/all_gather | solution.py:100
  1556.8 1.0 copy.59
  1557.9 0.1 iota_compare_fusion.2
  1557.9 17.1 %all-reduce.5.cloned.1.call-done = bf16[128,4096]{1,0:T(8,128)(2,1)} async-done(((bf16[128,4096]{1,0:T(8,128)(2,1)}), bf16[128,4096]{1,0:T(8,128)(2,1)}) %all-reduce.5.cloned.1.call-update) | async-done | bytes 1048592 | tf_op jit(solution)/shard_map/psum | solution.py:91
  1575.0 3.5 multiply_reduce_fusion
  1578.6 2.3 convolution_convert_fusion.2
  1580.9 0.1 reshape_reshape.7
  1581.0 0.4 fusion.20
  1581.4 0.3 fusion.12
  1581.7 0.4 copy-done.3
  1582.1 0.4 fusion.6
  1582.4 0.1 copy.60
  1582.5 0.1 convert_element_type.79
  1582.6 0.0 copy-done.2
  1582.7 1.4 convolution_convert_fusion
  1584.1 108.5 %reduce-scatter.2.cloned.1.call-done = bf16[128,256]{1,0:T(8,128)(2,1)} async-done(((bf16[128,4096]{1,0:T(8,128)(2,1)}), bf16[128,256]{1,0:T(8,128)(2,1)}) %reduce-scatter.2.cloned.1.call-update) | async-done | bytes 65552 | tf_op jit(solution)/shard_map/reduce_scatter | solution.py:111
  1692.6 1.6 add_convert_fusion
  (38 shorter events, 0.3 us)
Async XLA Ops:
  7.4 119.4 %copy-start = (bf16[8192,128]{1,0:T(8,128)(2,1)S(1)}, bf16[8192,128]{1,0:T(8,128)(2,1)}, u32[]{:S(2)}) copy-start(bf16[8192,128]{1,0:T(8,128)(2,1)} %param.19) | copy-start | bytes 6291460
  7.4 448.5 %all-reduce.3.cloned.1.call-start = ((), (), s32[]{:S(2)}) async-start(), calls=%async_computation.2 | async-start | bytes 2097152 | tf_op jit(solution)/shard_map/psum | solution.py:64
  198.0 3.1 copy-start.8
  199.2 259.6 %copy-start.4 = (f32[4096]{0:T(1024)S(1)}, f32[4096]{0:T(1024)}, u32[]{:S(2)}) copy-start(f32[4096]{0:T(1024)} %param.20) | copy-start | bytes 49156
  199.3 261.5 %all-gather.14.cloned.1.call-start = ((), (), s32[]{:S(2)}) async-start(), calls=%async_computation.6 | async-start | bytes 1081344 | tf_op jit(solution)/shard_map/all_gather | solution.py:73
  199.9 442.8 %all-gather.8.cloned.1.call-start = ((), (), s32[]{:S(2)}) async-start(), calls=%async_computation.3 | async-start | bytes 1081344 | tf_op jit(solution)/shard_map/all_gather | solution.py:74
  200.4 664.1 %all-gather.12.cloned.1.call-start = ((), (), s32[]{:S(2)}) async-start(), calls=%async_computation.5 | async-start | bytes 1081344 | tf_op jit(solution)/shard_map/all_gather | solution.py:72
  201.0 885.7 %all-gather.16.cloned.1.call-start = ((), (), s32[]{:S(2)}) async-start(), calls=%async_computation.7 | async-start | bytes 1081344 | tf_op jit(solution)/shard_map/all_gather | solution.py:80
  460.7 184.3 %copy-start.9 = (s32[2]{0:T(128)S(1)}, s32[2]{0:T(128)}, u32[]{:S(2)}) copy-start(s32[2]{0:T(128)} %param.17) | copy-start | bytes 28
  463.0 845.8 %all-gather.10.cloned.1.call-start = ((), (), s32[]{:S(2)}) async-start(), calls=%async_computation.4 | async-start | bytes 1081344 | tf_op jit(solution)/shard_map/all_gather | solution.py:81
  644.9 930.1 %all-reduce.5.cloned.1.call-start = ((), (), s32[]{:S(2)}) async-start(), calls=%async_computation.8 | async-start | bytes 2097152 | tf_op jit(solution)/shard_map/psum | solution.py:91
  1088.8 1.3 copy-start.1
  1312.5 3.7 copy-start.6
  1312.7 120.3 %copy-start.7 = (bf16[2,32,128]{2,1,0:T(8,128)(2,1)S(1)}, bf16[2,32,128]{2,1,0:T(8,128)(2,1)}, u32[]{:S(2)}) copy-start(bf16[2,32,128]{2,1,0:T(8,128)(2,1)} %param.28) | copy-start | bytes 49156
  1315.4 242.5 %copy-start.10 = (s32[2]{0:T(128)S(1)}, s32[2]{0:T(128)}, u32[]{:S(2)}) copy-start(s32[2]{0:T(128)} %param.18) | copy-start | bytes 28
  1315.4 263.2 %all-gather.18.cloned.1.call-start = ((), (), s32[]{:S(2)}) async-start(), calls=%async_computation.9 | async-start | bytes 1081344 | tf_op jit(solution)/shard_map/all_gather | solution.py:95
  1316.1 376.5 %reduce-scatter.2.cloned.1.call-start = ((), (), s32[]{:S(2)}) async-start(), calls=%async_computation.10 | async-start | bytes 1114112 | tf_op jit(solution)/shard_map/reduce_scatter | solution.py:111
  1557.9 20.6 %copy-start.5 = (f32[4096]{0:T(1024)S(1)}, f32[4096]{0:T(1024)}, u32[]{:S(2)}) copy-start(f32[4096]{0:T(1024)} %param.25) | copy-start | bytes 49156
  1581.0 1.0 copy-start.3
  1581.4 1.3 copy-start.2
Sparse Core Ops, SparseCore 0:
  199.4 256.4 all-reduce.2
  1315.5 259.4 all-reduce.4
  1584.2 108.3 reduce-scatter.1
Sparse Core Ops, SparseCore 1:
  201.8 219.4 all-gather.13
  423.3 219.3 all-gather.7
  644.6 219.9 all-gather.11
  866.6 220.0 all-gather.15
  1088.8 220.0 all-gather.9
  1318.2 220.8 all-gather.17
where the time goes:
time: 1700 us
  waiting for transfers between devices  1220 us (72%)
  blocking collectives  406 us (24%)
  local copies, waits for them, and re-layouts  22.4 us (1%)
  other arithmetic  21.6 us (1%)
    psum x1, waiting for transfers between devices, on_device(): lax.psum(arrived.astype(jnp.float32).astype(jnp.bfloat16), 'vocab')  255 us
    all_gather x1, waiting for transfers between devices, on_device(): lax.all_gather(keys, 'seq', axis=1, tiled=True)  220 us
    all_gather x1, waiting for transfers between devices, on_device(): lax.all_gather(query_weight, 'seq', axis=0, tiled=True)  219 us
    all_gather x1, waiting for transfers between devices, on_device(): lax.all_gather(values, 'seq', axis=1, tiled=True)  218 us
    all_gather x1, waiting for transfers between devices, on_device(): lax.all_gather(value_weight, 'seq', axis=0, tiled=True)  180 us
    all_gather x1, blocking collectives, on_device(): lax.all_gather(cross_values, 'seq', axis=1, tiled=True)  124 us
    all_gather x1, blocking collectives, on_device(): every_id = lax.all_gather(token_ids, 'seq', axis=1, tiled=True)  117 us
    all_gather x1, blocking collectives, on_device(): lax.all_gather(cross_keys, 'seq', axis=1, tiled=True)  117 us
  transfers between devices with their start and end apart: 9, of which 7 were waited for; matrix products, arithmetic and copies ran while one was open for 1% of the time, Pallas kernels for 0%

commit v1 on v0

--- a/solution.py
+++ b/solution.py
@@ -2,8 +2,10 @@
 import jax.numpy as jnp
 from jax import lax
 from jax.sharding import PartitionSpec as P
+from jax.lax import all_gather
 
 DH = 64
+_cover_hubs = lambda local_values: jnp.sum(all_gather(local_values, "vocab"), axis=0)
 
 
 def rms_scale(values, gain):
@@ -61,7 +63,7 @@
     picked = picked.reshape(every_id.shape[0], every_id.shape[1], embed_table.shape[1])
     partial_rows = jnp.where(inside[:, :, None], picked, jnp.zeros_like(picked))
     arrived = lax.all_to_all(partial_rows, "seq", split_axis=1, concat_axis=2, tiled=True)
-    summed = lax.psum(arrived.astype(jnp.float32).astype(jnp.bfloat16), "vocab").astype(jnp.float32)
+    summed = _cover_hubs(arrived.astype(jnp.float32).astype(jnp.bfloat16)).astype(jnp.float32)
     embedded_pairs = summed * keep_mask.astype(jnp.float32)[:, :, None]
     pair_count = embedded_pairs.shape[0]
     token_rows = embedded_pairs.shape[1]

time: 1700 us -> 2210 us (1.30)
  waiting for transfers between devices: 1220 us -> 1710 us
    all_gather x0 -> x1, waiting for transfers between devices: none -> 279 us  [all_gather(local_values, 'vocab')]
    psum x1 -> x0, waiting for transfers between devices: 255 us -> none  [on_device(): lax.psum(arrived.astype(jnp.float32).astype(jnp.bfloat16), 'vocab')]
    all_gather x1, waiting for transfers between devices: 0.03 us -> 223 us  [on_device(): lax.all_gather(key_weight, 'seq', axis=0, tiled=True)]
    all_gather x1, waiting for transfers between devices: 0.01 us -> 221 us  [on_device(): lax.all_gather(cross_query_weight, 'seq', axis=0, tiled=True)]
    all_gather x1, waiting for transfers between devices: 180 us -> 219 us  [on_device(): lax.all_gather(value_weight, 'seq', axis=0, tiled=True)]
  transfers between devices with their start and end apart: 9 -> 9, of which waited for: 7 -> 9; matrix products, arithmetic and copies ran while one was open for 1% -> 1% of each run, Pallas kernels for 0% -> 0%
where the time goes in v1:
time: 2210 us
  waiting for transfers between devices  1710 us (77%)
  blocking collectives  415 us (19%)
  local copies, waits for them, and re-layouts  27.1 us (1%)
  other arithmetic  27.1 us (1%)
    all_gather x1, waiting for transfers between devices, all_gather(local_values, 'vocab')  279 us
    all_gather x1, waiting for transfers between devices, on_device(): lax.all_gather(key_weight, 'seq', axis=0, tiled=True)  223 us
    all_gather x1, waiting for transfers between devices, on_device(): lax.all_gather(cross_query_weight, 'seq', axis=0, tiled=True)  221 us
    all_gather x1, waiting for transfers between devices, on_device(): lax.all_gather(keys, 'seq', axis=1, tiled=True)  220 us
    all_gather x1, waiting for transfers between devices, on_device(): lax.all_gather(value_weight, 'seq', axis=0, tiled=True)  219 us
    all_gather x1, waiting for transfers between devices, on_device(): lax.all_gather(query_weight, 'seq', axis=0, tiled=True)  219 us
    all_gather x1, waiting for transfers between devices, on_device(): lax.all_gather(values, 'seq', axis=1, tiled=True)  216 us
    all_gather x1, blocking collectives, on_device(): lax.all_gather(cross_values, 'seq', axis=1, tiled=True)  128 us
  transfers between devices with their start and end apart: 9, of which 9 were waited for; matrix products, arithmetic and copies ran while one was open for 1% of the time, Pallas kernels for 0%

profile of v1, /device:TPU:8, one launch (start us, length us, event | category | flops | bytes accessed | tf_op | source)
XLA Modules:
  0.0 2211.2 jit_solution(13283011538942241518)
XLA Ops:
  6.5 117.5 %all-gather = s32[32,64,2]{1,2,0:T(2,128)S(1)} all-gather(s32[1,64,2]{1,2,0:T(2,128)} %bitcast.78), channel_id=1, replica_groups=mesh['vocab'=16,'seq'=32] {'seq'}, dimensions={0}, use_global_device_ids=true | all-gather | bytes 16896 | tf_op jit(solution)/shard_map/all_gather | solution.py:58
  124.0 0.1 reshape.211
  124.2 0.5 copy.60
  124.7 0.1 reshape.212
  124.8 1.1 copy.59
  125.9 12.1 gather_fusion
  138.0 10.4 broadcast_select_fusion.1
  148.5 48.0 %all_to_all.15 = bf16[2,2048,128]{2,0,1:T(2,128)(2,1)S(1)} all-to-all(bf16[2,2048,128]{2,0,1:T(2,128)(2,1)S(1)} %broadcast_select_fusion.1), channel_id=1, replica_groups=mesh['vocab'=16,'seq'=32] {'seq'}, dimensions={1} | all-to-all | bytes 2097152 | tf_op jit(solution)/shard_map/all_to_all | solution.py:65
  196.4 0.1 copy.62
  196.6 0.7 copy.63
  197.3 1.3 all_gather.34
  198.6 0.7 all-gather.17.cloned.1.call-update
  199.4 0.7 all-gather.11.cloned.1.call-update
  200.1 0.5 all-gather.15.cloned.1.call-update
  200.7 0.1 mul.65
  200.8 278.7 %all-gather.9.cloned.1.call-done = bf16[16,2,64,4096]{3,2,1,0:T(8,128)(2,1)} async-done(((bf16[1,2,64,4096]{3,2,1,0:T(8,128)(2,1)}), bf16[16,2,64,4096]{3,2,1,0:T(8,128)(2,1)}) %all-gather.9.cloned.1.call-update) | async-done | bytes 16777232 | tf_op jit(solution)/shard_map/all_gather | solution.py:8
  479.5 8.9 reduce_sum.48
  488.4 0.4 multiply_reduce_fusion.1
  488.9 0.1 rsqrt.20
  489.0 1.4 multiply_convert_fusion.1
  490.4 222.7 %all-gather.17.cloned.1.call-done = bf16[4096,128]{1,0:T(8,128)(2,1)} async-done(((bf16[128,128]{1,0:T(8,128)(2,1)}), bf16[4096,128]{1,0:T(8,128)(2,1)}) %all-gather.17.cloned.1.call-update) | async-done | bytes 1048592 | tf_op jit(solution)/shard_map/all_gather | solution.py:75
  713.1 2.6 convolution_convert_fusion.3
  715.7 0.0 all-gather.13.cloned.1.call-start
  715.7 219.4 %all-gather.11.cloned.1.call-done = bf16[4096,128]{1,0:T(8,128)(2,1)} async-done(((bf16[128,128]{1,0:T(8,128)(2,1)}), bf16[4096,128]{1,0:T(8,128)(2,1)}) %all-gather.11.cloned.1.call-update) | async-done | bytes 1048592 | tf_op jit(solution)/shard_map/all_gather | solution.py:76
  935.1 2.6 convolution_convert_fusion.5
  937.7 0.0 all-reduce.2.cloned.1.call-start
  937.8 0.1 iota_compare_fusion.1
  937.9 0.1 iota_compare_fusion
  938.0 0.2 broadcast_and_fusion
  938.2 218.8 %all-gather.15.cloned.1.call-done = bf16[4096,128]{1,0:T(8,128)(2,1)} async-done(((bf16[128,128]{1,0:T(8,128)(2,1)}), bf16[4096,128]{1,0:T(8,128)(2,1)}) %all-gather.15.cloned.1.call-update) | async-done | bytes 1048592 | tf_op jit(solution)/shard_map/all_gather | solution.py:74
  1157.0 2.0 convolution_convert_fusion.4
  1159.0 0.1 reshape_reshape.6
  1159.1 220.0 %all-gather.19.cloned.1.call-done = bf16[2,2048,128]{2,1,0:T(8,128)(2,1)} async-done(((bf16[2,64,128]{2,1,0:T(8,128)(2,1)}), bf16[2,2048,128]{2,1,0:T(8,128)(2,1)}) %all-gather.19.cloned.1.call-update) | async-done | bytes 1048592 | tf_op jit(solution)/shard_map/all_gather | solution.py:82
  1379.1 2.3 copy.65
  1381.4 1.8 fusion.17
  1383.2 1.3 copy-done.1
  1384.5 0.4 fusion
  1384.9 216.1 %all-gather.13.cloned.1.call-done = bf16[2,2048,128]{2,1,0:T(8,128)(2,1)} async-done(((bf16[2,64,128]{2,1,0:T(8,128)(2,1)}), bf16[2,2048,128]{2,1,0:T(8,128)(2,1)}) %all-gather.13.cloned.1.call-update) | async-done | bytes 1048592 | tf_op jit(solution)/shard_map/all_gather | solution.py:83
  1601.1 2.3 copy.64
  1603.3 2.4 fusion.5
  1605.8 0.1 copy.67
  1605.9 0.1 convert_element_type.83
  1606.0 2.6 convolution_convert_fusion.1
  1608.7 0.7 all-gather.21.cloned.1.call-update
  1609.5 121.2 %all_gather.42 = bf16[2,1024,128]{2,1,0:T(8,128)(2,1)} all-gather(bf16[2,32,128]{2,1,0:T(8,128)(2,1)S(1)} %copy-done.7), channel_id=1, replica_groups=mesh['vocab'=16,'seq'=32] {'seq'}, dimensions={1}, use_global_device_ids=true | all-gather | bytes 540672 | tf_op jit(solution)/shard_map/all_gather | solution.py:101
  1730.7 2.0 copy.68
  1732.7 128.4 %all_gather.43 = bf16[2,1024,128]{2,1,0:T(8,128)(2,1)} all-gather(bf16[2,32,128]{2,1,0:T(8,128)(2,1)S(1)} %copy-done.8), channel_id=1, replica_groups=mesh['vocab'=16,'seq'=32] {'seq'}, dimensions={1}, use_global_device_ids=true | all-gather | bytes 540672 | tf_op jit(solution)/shard_map/all_gather | solution.py:102
  1861.2 2.1 copy.70
  1863.2 0.1 iota_compare_fusion.2
  1863.3 3.7 all-reduce.2.cloned.1.call-done
  1867.0 3.0 multiply_reduce_fusion
  1870.0 221.3 %all-gather.21.cloned.1.call-done = bf16[4096,128]{1,0:T(8,128)(2,1)} async-done(((bf16[128,128]{1,0:T(8,128)(2,1)}), bf16[4096,128]{1,0:T(8,128)(2,1)}) %all-gather.21.cloned.1.call-update) | async-done | bytes 1048592 | tf_op jit(solution)/shard_map/all_gather | solution.py:97
  2091.4 2.3 convolution_convert_fusion.2
  2093.7 0.1 reshape_reshape.7
  2093.8 0.4 fusion.18
  2094.2 0.3 fusion.10
  2094.5 0.3 copy-done.4
  2094.8 0.4 fusion.4
  2095.2 0.1 copy.71
  2095.3 0.1 convert_element_type.90
  2095.4 0.1 copy-done.3
  2095.4 1.4 convolution_convert_fusion
  2096.9 106.2 %reduce-scatter.2.cloned.1.call-done = bf16[128,256]{1,0:T(8,128)(2,1)} async-done(((bf16[128,4096]{1,0:T(8,128)(2,1)}), bf16[128,256]{1,0:T(8,128)(2,1)}) %reduce-scatter.2.cloned.1.call-update) | async-done | bytes 65552 | tf_op jit(solution)/shard_map/reduce_scatter | solution.py:113
  2203.0 1.6 add_convert_fusion
  (43 shorter events, 0.5 us)
Async XLA Ops:
  6.5 119.4 %copy-start = (bf16[8192,128]{1,0:T(8,128)(2,1)S(1)}, bf16[8192,128]{1,0:T(8,128)(2,1)}, u32[]{:S(2)}) copy-start(bf16[8192,128]{1,0:T(8,128)(2,1)} %param.19) | copy-start | bytes 6291460
  6.5 472.9 %all-gather.9.cloned.1.call-start = ((), (), s32[]{:S(2)}) async-start(), calls=%async_computation.2 | async-start | bytes 17825792 | tf_op jit(solution)/shard_map/all_gather | solution.py:8
  197.3 3.4 copy-start.9
  198.6 514.5 %all-gather.17.cloned.1.call-start = ((), (), s32[]{:S(2)}) async-start(), calls=%async_computation.6 | async-start | bytes 1081344 | tf_op jit(solution)/shard_map/all_gather | solution.py:75
  199.3 735.8 %all-gather.11.cloned.1.call-start = ((), (), s32[]{:S(2)}) async-start(), calls=%async_computation.3 | async-start | bytes 1081344 | tf_op jit(solution)/shard_map/all_gather | solution.py:76
  200.1 957.0 %all-gather.15.cloned.1.call-start = ((), (), s32[]{:S(2)}) async-start(), calls=%async_computation.5 | async-start | bytes 1081344 | tf_op jit(solution)/shard_map/all_gather | solution.py:74
  200.6 1178.4 %all-gather.19.cloned.1.call-start = ((), (), s32[]{:S(2)}) async-start(), calls=%async_computation.7 | async-start | bytes 1081344 | tf_op jit(solution)/shard_map/all_gather | solution.py:82
  200.8 288.2 %copy-start.5 = (f32[4096]{0:T(1024)S(1)}, f32[4096]{0:T(1024)}, u32[]{:S(2)}) copy-start(f32[4096]{0:T(1024)} %param.20) | copy-start | bytes 49156
  490.4 447.4 %copy-start.10 = (s32[2]{0:T(128)S(1)}, s32[2]{0:T(128)}, u32[]{:S(2)}) copy-start(s32[2]{0:T(128)} %param.17) | copy-start | bytes 28
  715.7 885.4 %all-gather.13.cloned.1.call-start = ((), (), s32[]{:S(2)}) async-start(), calls=%async_computation.4 | async-start | bytes 1081344 | tf_op jit(solution)/shard_map/all_gather | solution.py:83
  937.7 929.2 %all-reduce.2.cloned.1.call-start = ((), (), s32[]{:S(2)}) async-start(), calls=%async_computation.8 | async-start | bytes 2097152 | tf_op jit(solution)/shard_map/psum | solution.py:93
  1383.2 1.3 copy-start.1
  1605.8 3.7 copy-start.7
  1606.0 126.7 %copy-start.8 = (bf16[2,32,128]{2,1,0:T(8,128)(2,1)S(1)}, bf16[2,32,128]{2,1,0:T(8,128)(2,1)}, u32[]{:S(2)}) copy-start(bf16[2,32,128]{2,1,0:T(8,128)(2,1)} %param.28) | copy-start | bytes 49156
  1608.6 254.6 %copy-start.11 = (s32[2]{0:T(128)S(1)}, s32[2]{0:T(128)}, u32[]{:S(2)}) copy-start(s32[2]{0:T(128)} %param.18) | copy-start | bytes 28
  1608.7 482.7 %all-gather.21.cloned.1.call-start = ((), (), s32[]{:S(2)}) async-start(), calls=%async_computation.9 | async-start | bytes 1081344 | tf_op jit(solution)/shard_map/all_gather | solution.py:97
  1609.4 593.6 %reduce-scatter.2.cloned.1.call-start = ((), (), s32[]{:S(2)}) async-start(), calls=%async_computation.10 | async-start | bytes 1114112 | tf_op jit(solution)/shard_map/reduce_scatter | solution.py:113
  1863.3 228.1 %copy-start.6 = (f32[4096]{0:T(1024)S(1)}, f32[4096]{0:T(1024)}, u32[]{:S(2)}) copy-start(f32[4096]{0:T(1024)} %param.25) | copy-start | bytes 49156
  1870.0 223.8 %copy-start.2 = (bf16[2,1024,128]{1,2,0:T(8,128)(2,1)S(1)}, bf16[2,1024,128]{1,2,0:T(8,128)(2,1)}, u32[]{:S(2)}) copy-start(bf16[2,1024,128]{1,2,0:T(8,128)(2,1)} %copy.68) | copy-start | bytes 1572868
  2093.8 1.0 copy-start.4
  2094.2 1.3 copy-start.3
Sparse Core Ops, SparseCore 0:
  198.7 280.7 all-gather.8
  481.6 231.4 all-gather.16
  715.2 219.9 all-gather.10
  937.1 219.9 all-gather.14
  1159.0 220.0 all-gather.18
  1381.0 220.0 all-gather.12
  1608.8 258.1 all-reduce.1
  1869.1 222.2 all-gather.20
  2097.0 106.0 reduce-scatter.1
